TPU v7x, 512 devices: a whole 4x8x8 slice. The times are simulated.
512 devices in a mesh: coil: 32 (over x, y), slab: 16 (over z, core).
Axes of the slice: x: 4, y: 8, z: 8, core: 2. Of those that a mesh axis runs over, the one named last changes fastest.
Arguments:
- adjoint_data: float32 [16, 192, 384], P('slab', 'coil'), may hold values from -80 to 80
- denoised: float32 [16, 192, 384], P('slab', 'coil'), may hold values from -8 to 8, as said below
- sensitivity: float32 [32, 16, 192, 384], P('coil', 'slab'), may hold values from -2 to 2, as said below
- kernel: float32 [16, 384, 384], P(None, 'slab'), may hold values from 0.1 to 2, as said below
- conv_in: bfloat16 [54, 64], replicated, may hold values from -0.875 to 0.875
- conv_mid: bfloat16 [1728, 64], replicated, may hold values from -0.15625 to 0.15625
- conv_out: bfloat16 [1728, 2], replicated, may hold values from -0.15625 to 0.15625
Outputs:
- solution: float32 [16, 192, 384], P('slab', 'coil')
- refined: float32 [16, 192, 384], P('slab', 'coil')
Inputs may be any that keep to these rules, and one draw needn't show every extreme that they name: `denoised`: real and imaginary parts of the previous cascade's image. `sensitivity`: real and imaginary parts of the coil maps. Positive kernel values.
All inputs are finite; a program needn't handle non-finite values.
Results may differ from a plain program's by a relative error of at most 0.0023.
Values may be sent and summed in bfloat16 or wider, within the bound.
A program may use at most 64 MiB of HBM per device.

v0:
```python
import math

import jax
import jax.numpy as jnp
from jax import lax
from jax.sharding import PartitionSpec as P

ITERS = 2


reg_weight = 0.5
highest = lax.Precision.HIGHEST


def with_halo(cells, sides, width):
    for axis, dim in sides:
        count = lax.axis_size(axis)
        ends = count - 1
        head = lax.slice_in_dim(cells, 0, width, axis=dim)
        tail = lax.slice_in_dim(cells, cells.shape[dim] - width, cells.shape[dim], axis=dim)
        cells = jnp.concatenate(
            [
                lax.ppermute(tail, axis, [(i, (i + 1) % count) for i in range(ends)]),
                cells,
                lax.ppermute(head, axis, [((i + 1) % count, i) for i in range(ends)]),
            ],
            axis=dim,
        )
    return cells


def dft_tables(out_len, in_len, length, inverse):
    out_index = lax.broadcasted_iota(jnp.int32, (out_len, in_len), 0)
    in_index = lax.broadcasted_iota(jnp.int32, (out_len, in_len), 1)
    phases = (out_index * in_index % length).astype(jnp.float32) * (2.0 * math.pi / length)
    if inverse:
        return (jnp.cos(phases) / length, jnp.sin(phases) / length)
    return (jnp.cos(phases), -jnp.sin(phases))


def block_matrix(tables):
    cos_table = tables[0]
    sin_table = tables[1]
    upper = jnp.concatenate([cos_table.T, sin_table.T], axis=1)
    lower = jnp.concatenate([-sin_table.T, cos_table.T], axis=1)
    return jnp.concatenate([upper, lower], axis=0)


def along_axis(values, tables, einsum_form):
    half_len = values.shape[-1] // 2
    real_part = jnp.einsum(einsum_form, tables[0], values, precision=highest)
    imag_part = jnp.einsum(einsum_form, tables[1], values, precision=highest)
    return jnp.concatenate(
        [
            real_part[..., :half_len] - imag_part[..., half_len:],
            real_part[..., half_len:] + imag_part[..., :half_len],
        ],
        axis=-1,
    )


def complex_product(factor_one, factor_two):
    half_len = factor_one.shape[-1] // 2
    real_one = factor_one[..., :half_len]
    imag_one = factor_one[..., half_len:]
    real_two = factor_two[..., :half_len]
    imag_two = factor_two[..., half_len:]
    return jnp.concatenate(
        [real_one * real_two - imag_one * imag_two, real_one * imag_two + imag_one * real_two],
        axis=-1,
    )


def conj_product(factor_one, factor_two):
    half_len = factor_one.shape[-1] // 2
    real_one = factor_one[..., :half_len]
    imag_one = factor_one[..., half_len:]
    real_two = factor_two[..., :half_len]
    imag_two = factor_two[..., half_len:]
    return jnp.concatenate(
        [real_one * real_two + imag_one * imag_two, real_one * imag_two - imag_one * real_two],
        axis=-1,
    )


def convolve(features, weights, in_channels):
    padded = with_halo(features, (("coil", 1), ("slab", 0)), 1)
    depth_here = features.shape[0]
    rows_here = features.shape[1]
    side_len = features.shape[2] // in_channels
    padded_cube = padded.reshape(depth_here + 2, rows_here + 2, side_len, in_channels)
    padded_cube = jnp.pad(padded_cube, ((0, 0), (0, 0), (1, 1), (0, 0)))
    width_taps = 9 * in_channels
    running = None
    for shift_z in range(3):
        tap_list = [
            padded_cube[
                shift_z : shift_z + depth_here,
                shift_x : shift_x + rows_here,
                shift_y : shift_y + side_len,
                :,
            ]
            for shift_x in range(3)
            for shift_y in range(3)
        ]
        patches = jnp.concatenate(tap_list, axis=-1).reshape(-1, width_taps)
        partial_sum = jnp.dot(
            patches,
            weights[shift_z * width_taps : (shift_z + 1) * width_taps],
            preferred_element_type=jnp.float32,
        )
        running = partial_sum if shift_z == 0 else running + partial_sum
    return running


def shards(adjoint_data, denoised, sensitivity, kernel, conv_in, conv_mid, conv_out):
    side_len = sensitivity.shape[2]
    depth_len = kernel.shape[0]
    grid_len = kernel.shape[2]
    fwd_plane = dft_tables(grid_len, side_len, grid_len, False)
    inv_plane = dft_tables(side_len, grid_len, grid_len, True)
    fwd_depth = dft_tables(depth_len, depth_len, depth_len, False)
    inv_depth = dft_tables(depth_len, depth_len, depth_len, True)
    fwd_last = block_matrix(fwd_plane)
    inv_last = block_matrix(inv_plane)

    def total_squares(residual):
        return lax.psum(jnp.sum(residual * residual), ("coil", "slab"))

    right_side = adjoint_data + reg_weight * denoised
    solution = jnp.zeros_like(right_side)
    residual = right_side
    direction = right_side
    norm_now = total_squares(residual)
    for iteration in range(ITERS):
        products = complex_product(
            sensitivity, lax.all_gather(direction, "coil", axis=1, tiled=True)[None]
        )
        products = jnp.matmul(products, fwd_last, precision=highest)
        spread = along_axis(products, fwd_plane, "kn,cznw->czkw")
        apply_pencil = lax.all_to_all(spread, "slab", split_axis=2, concat_axis=1, tiled=True)
        spectrum = along_axis(apply_pencil, fwd_depth, "kn,cnxw->ckxw")
        shape_now = spectrum.shape
        split_form = spectrum.reshape(shape_now[0], shape_now[1], shape_now[2], 2, grid_len)
        weighted = split_form * kernel[None, :, :, None, :]
        returned = along_axis(weighted.reshape(shape_now), inv_depth, "kn,cnxw->ckxw")
        slab_back = lax.all_to_all(returned, "slab", split_axis=1, concat_axis=2, tiled=True)
        image_back = along_axis(slab_back, inv_plane, "kn,cznw->czkw")
        image_back = jnp.matmul(image_back, inv_last, precision=highest)
        coil_sum = jnp.sum(conj_product(sensitivity, image_back), axis=0)
        summed = lax.psum_scatter(coil_sum, "coil", scatter_dimension=1, tiled=True)
        image_out = summed + reg_weight * direction
        local_curv = jnp.sum(direction * image_out)
        image_out, local_curv = (image_out, local_curv)
        curvature = lax.psum(local_curv, ("coil", "slab"))
        step_size = norm_now / curvature
        solution = solution + step_size * direction
        if iteration + 1 < ITERS:
            residual = residual - step_size * image_out
            norm_next = total_squares(residual)
            direction = residual + norm_next / norm_now * direction
            norm_now = norm_next
    depth_here = solution.shape[0]
    rows_here = solution.shape[1]
    channels = jnp.stack([solution[..., :side_len], solution[..., side_len:]], axis=-1).astype(
        jnp.bfloat16
    )
    first_map = convolve(channels.reshape(depth_here, rows_here, 2 * side_len), conv_in, 2)
    hidden_count = conv_mid.shape[1]
    hidden_one = (
        jax.nn.relu(first_map)
        .astype(jnp.bfloat16)
        .reshape(depth_here, rows_here, side_len * hidden_count)
    )
    second_map = convolve(hidden_one, conv_mid, hidden_count)
    hidden_two = (
        jax.nn.relu(second_map)
        .astype(jnp.bfloat16)
        .reshape(depth_here, rows_here, side_len * hidden_count)
    )
    third_map = convolve(hidden_two, conv_out, hidden_count).reshape(
        depth_here, rows_here, side_len, 2
    )
    refined = solution + jnp.concatenate([third_map[..., 0], third_map[..., 1]], axis=-1)
    return (solution, refined)


def solution(mesh):
    placed = (
        P("slab", "coil", None),
        P("slab", "coil", None),
        P("coil", "slab", None, None),
        P(None, "slab", None),
        P(),
        P(),
        P(),
    )
    return jax.shard_map(
        shards,
        mesh=mesh,
        in_specs=placed,
        out_specs=(P("slab", "coil", None), P("slab", "coil", None)),
        check_vma=False,
    )
```

profile of v0, /device:TPU:1, one launch (start us, length us, event | category | flops | bytes accessed | tf_op | source)
XLA Modules:
  0.0 1026.6 jit_solution(9897725327793448658)
XLA Ops:
  10.4 39.4 %all_gather.6 = f32[1,192,384]{2,0,1:T(1,128)S(1)} all-gather(f32[1,6,384]{2,0,1:T(1,128)S(1)} %copy.111), channel_id=1, replica_groups=mesh['coil'=32,'slab'=16] {'coil'}, dimensions={1}, use_global_device_ids=true | all-gather | bytes 304128 | tf_op jit(solution)/shard_map/all_gather | solution.py:137
  51.2 4.0 convolution_bitcast_fusion.10
  55.2 4.0 convolution_bitcast_fusion.11
  59.4 2.7 copy.112
  62.1 23.9 %all-to-all-start = ((f32[1,1,384,768]{3,1,0,2:T(1,128)}), f32[1,1,384,768]{3,1,0,2:T(1,128)S(1)}, u32[]{:S(2)}, u32[]{:S(2)}) async-start(f32[1,1,384,768]{3,1,0,2:T(1,128)} %copy.112), calls=%async_computation | async-start | bytes 2359296 | tf_op jit(solution)/shard_map/all_to_all | solution.py:141
  86.2 1.7 mul.249
  87.8 2.2 mul.250
  90.1 26.5 %all-to-all-done = f32[1,1,384,768]{3,1,0,2:T(1,128)S(1)} async-done(((f32[1,1,384,768]{3,1,0,2:T(1,128)}), f32[1,1,384,768]{3,1,0,2:T(1,128)S(1)}, u32[]{:S(2)}, u32[]{:S(2)}) %all-to-all-start) | async-done | bytes 1179680 | tf_op jit(solution)/shard_map/all_to_all | solution.py:141
  116.7 1.4 convolution_bitcast_fusion.6
  118.1 1.4 convolution_bitcast_fusion.7
  122.4 1.7 copy.116
  124.2 3.6 all-to-all-start.1
  128.0 1.5 fusion.59
  129.5 2.4 fusion.25
  131.9 26.5 %all-to-all-done.1 = f32[1,16,24,768]{3,2,0,1:T(8,128)S(1)} async-done(((f32[1,16,24,768]{3,2,0,1:T(8,128)}), f32[1,16,24,768]{3,2,0,1:T(8,128)S(1)}, u32[]{:S(2)}, u32[]{:S(2)}) %all-to-all-start.1) | async-done | bytes 1179680 | tf_op jit(solution)/shard_map/all_to_all | solution.py:147
  158.4 2.3 convolution_bitcast_fusion.14
  160.7 2.3 convolution_bitcast_fusion.15
  168.8 144.3 %all-reduce.9.cloned.1.call-done = f32[1,192,384]{2,0,1:T(1,128)} async-done(((f32[1,192,384]{2,0,1:T(1,128)}), f32[1,192,384]{2,0,1:T(1,128)}) %all-reduce.9.cloned.1.call-update) | async-done | bytes 294928
  314.4 100.7 %all-reduce.5 = (f32[]{:T(128)}, f32[]{:T(128)}) all-reduce(f32[]{:T(128)} %get-tuple-element.13, f32[]{:T(128)} %get-tuple-element.12), channel_id=1, replica_groups=mesh['coil'=32,'slab'=16] {'coil','slab'}, use_global_device_ids=true, to_apply=%region_1.2 | all-reduce | flops 2 | bytes 16 | tf_op jit(solution)/shard_map/psum | solution.py:128
  417.1 94.7 %psum.30 = f32[]{:T(128)} all-reduce(f32[]{:T(128)} %multiply_reduce_fusion), channel_id=1, replica_groups=mesh['coil'=32,'slab'=16] {'coil','slab'}, use_global_device_ids=true, to_apply=%region_6.7 | all-reduce | flops 1 | bytes 8 | tf_op jit(solution)/shard_map/psum | solution.py:128
  513.2 36.0 %all_gather.7 = f32[1,192,384]{2,0,1:T(1,128)S(1)} all-gather(f32[1,6,384]{2,0,1:T(1,128)S(1)} %copy.119), channel_id=1, replica_groups=mesh['coil'=32,'slab'=16] {'coil'}, dimensions={1}, use_global_device_ids=true | all-gather | bytes 304128 | tf_op jit(solution)/shard_map/all_gather | solution.py:137
  550.6 4.0 convolution_bitcast_fusion.8
  554.6 4.0 convolution_bitcast_fusion.9
  558.7 2.7 copy.120
  561.5 49.7 %all_to_all.16 = f32[1,1,384,768]{3,1,0,2:T(1,128)S(1)} all-to-all(f32[1,1,384,768]{3,1,0,2:T(1,128)} %copy.120), channel_id=1, replica_groups=mesh['coil'=32,'slab'=16] {'slab'}, dimensions={2} | all-to-all | bytes 2359296 | tf_op jit(solution)/shard_map/all_to_all | solution.py:141
  611.2 1.4 convolution_bitcast_fusion.2
  612.7 1.4 convolution_bitcast_fusion.3
  617.7 34.2 %all_to_all.17 = f32[1,16,24,768]{3,2,0,1:T(8,128)S(1)} all-to-all(f32[1,16,24,768]{3,2,0,1:T(8,128)S(1)} %copy.123), channel_id=1, replica_groups=mesh['coil'=32,'slab'=16] {'slab'}, dimensions={1} | all-to-all | bytes 2359296 | tf_op jit(solution)/shard_map/all_to_all | solution.py:147
  651.9 2.3 convolution_bitcast_fusion.12
  654.2 2.3 convolution_bitcast_fusion.13
  660.2 146.0 %all-reduce.11.cloned.1.call-done = f32[1,192,384]{2,0,1:T(1,128)} async-done(((f32[1,192,384]{2,0,1:T(1,128)}), f32[1,192,384]{2,0,1:T(1,128)}) %all-reduce.11.cloned.1.call-update) | async-done | bytes 294928
  807.5 100.6 %psum.31 = f32[]{:T(128)} all-reduce(f32[]{:T(128)} %fusion.74), channel_id=1, replica_groups=mesh['coil'=32,'slab'=16] {'coil','slab'}, use_global_device_ids=true, to_apply=%region_9.10 | all-reduce | flops 1 | bytes 8 | tf_op jit(solution)/shard_map/psum | solution.py:155
  909.8 2.3 collective-permute-start
  913.8 3.7 collective-permute-done.1
  917.6 4.0 collective-permute-start.3
  921.6 2.9 collective-permute-start.2
  925.2 1.5 fusion.193
  926.7 1.6 fusion.192
  928.4 4.2 concatenate.143
  933.3 1.7 concatenate.142
  935.8 1.7 concatenate.141
  939.6 2.9 collective-permute-start.4
  943.8 3.5 collective-permute-done.5
  947.5 3.5 collective-permute-start.7
  951.0 4.2 collective-permute-start.6
  960.3 1.7 pad_slice_fusion.18
  962.0 2.0 pad_slice_fusion.19
  963.9 3.1 concatenate.146
  967.0 2.2 fusion.71
  969.2 2.7 concatenate.147
  971.9 2.4 convolution_add_fusion.1
  974.3 2.9 concatenate.148
  977.2 1.5 fusion.3
  979.3 4.2 collective-permute-start.8
  984.8 3.8 collective-permute-done.9
  988.8 1.9 collective-permute-start.11
  990.7 5.5 collective-permute-start.10
  1001.5 1.7 pad_slice_fusion
  1003.2 2.0 pad_slice_fusion.1
  1005.2 3.1 concatenate.151
  1008.2 1.8 fusion.115
  1010.1 2.7 concatenate.152
  1012.8 1.8 convolution_add_fusion.5
  1014.6 2.9 concatenate.153
  (128 shorter events, 47.2 us)
Async XLA Ops:
  7.2 42.7 %copy-start = (f32[1,1,192,384]{3,2,1,0:T(8,128)S(1)}, f32[1,1,192,384]{3,2,1,0:T(8,128)}, u32[]{:S(2)}) copy-start(f32[1,1,192,384]{3,2,1,0:T(8,128)} %param.9) | copy-start | bytes 884740
  8.3 41.7 %copy-start.5 = (f32[192,384]{1,0:T(8,128)}, f32[192,384]{1,0:T(8,128)S(1)}, u32[]{:S(2)}) copy-start(f32[192,384]{1,0:T(8,128)S(1)} %fusion.66) | copy-start | bytes 884740
  9.5 41.7 %copy-start.7 = (f32[192,384]{1,0:T(8,128)}, f32[192,384]{1,0:T(8,128)S(1)}, u32[]{:S(2)}) copy-start(f32[192,384]{1,0:T(8,128)S(1)} %get-tuple-element.133) | copy-start | bytes 884740
  9.5 41.7 %copy-start.9 = (f32[192,384]{1,0:T(8,128)}, f32[192,384]{1,0:T(8,128)S(1)}, u32[]{:S(2)}) copy-start(f32[192,384]{1,0:T(8,128)S(1)} %get-tuple-element.134) | copy-start | bytes 884740
  62.1 23.9 %copy-start.2 = (f32[16,24,384]{2,1,0:T(8,128)S(1)}, f32[16,24,384]{2,1,0:T(8,128)}, u32[]{:S(2)}) copy-start(f32[16,24,384]{2,1,0:T(8,128)} %param.10) | copy-start | bytes 1769476
  62.1 54.4 %all-to-all-start = ((f32[1,1,384,768]{3,1,0,2:T(1,128)}), f32[1,1,384,768]{3,1,0,2:T(1,128)S(1)}, u32[]{:S(2)}, u32[]{:S(2)}) async-start(f32[1,1,384,768]{3,1,0,2:T(1,128)} %copy.112), calls=%async_computation | async-start | bytes 2359296 | tf_op jit(solution)/shard_map/all_to_all | solution.py:141
  124.2 34.2 %all-to-all-start.1 = ((f32[1,16,24,768]{3,2,0,1:T(8,128)}), f32[1,16,24,768]{3,2,0,1:T(8,128)S(1)}, u32[]{:S(2)}, u32[]{:S(2)}) async-start(f32[1,16,24,768]{3,2,0,1:T(8,128)} %copy.116), calls=%async_computation.1 | async-start | bytes 2359296 | tf_op jit(solution)/shard_map/all_to_all | solution.py:147
  127.8 185.3 %all-reduce.9.cloned.1.call-start = ((), (), s32[]{:S(2)}) async-start(), calls=%async_computation.4 | async-start | bytes 589824
  163.1 1.0 copy-start.3
  166.7 382.7 %copy-start.6 = (f32[192,384]{1,0:T(8,128)S(1)}, f32[192,384]{1,0:T(8,128)}, u32[]{:S(2)}) copy-start(f32[192,384]{1,0:T(8,128)} %copy-done.5) | copy-start | bytes 884740
  166.7 382.7 %copy-start.8 = (f32[192,384]{1,0:T(8,128)S(1)}, f32[192,384]{1,0:T(8,128)}, u32[]{:S(2)}) copy-start(f32[192,384]{1,0:T(8,128)} %copy-done.7) | copy-start | bytes 884740
  166.7 382.7 %copy-start.10 = (f32[192,384]{1,0:T(8,128)S(1)}, f32[192,384]{1,0:T(8,128)}, u32[]{:S(2)}) copy-start(f32[192,384]{1,0:T(8,128)} %copy-done.9) | copy-start | bytes 884740
  166.8 639.4 %all-reduce.11.cloned.1.call-start = ((), (), s32[]{:S(2)}) async-start(), calls=%async_computation.5 | async-start | bytes 589824
  656.5 1.0 copy-start.4
  909.8 3.9 collective-permute-start
  912.1 5.4 collective-permute-start.1
  917.6 6.9 collective-permute-start.3
  921.6 3.4 collective-permute-start.2
  937.5 0.8 copy-start.12
  939.6 4.2 collective-permute-start.4
  942.5 4.8 collective-permute-start.5
  947.5 8.9 collective-permute-start.7
  951.0 6.6 collective-permute-start.6
  974.3 2.9 copy-start.1
  979.3 5.5 collective-permute-start.8
  983.5 5.1 collective-permute-start.9
  988.8 8.9 collective-permute-start.11
  990.7 8.1 collective-permute-start.10
  1014.6 2.9 copy-start.11
Sparse Core Ops, SparseCore 0:
  166.8 146.2 all-reduce.8
  660.3 145.7 all-reduce.10
where the time goes:
time: 1030 us
  blocking collectives  455 us (44%)
  waiting for transfers between devices  359 us (35%)
  local copies, waits for them, and re-layouts  64.6 us (6%)
  starting transfers between devices  63.1 us (6%)
  matrix products  52.4 us (5%)
  between operations  19.8 us (2%)
  other arithmetic  12 us (1%)
    unnamed x4, waiting for transfers between devices  290 us
    psum x2, blocking collectives, total_squares(): return lax.psum(jnp.sum(residual * residual), ('coil', 'slab'))  195 us
    psum x1, blocking collectives, shards(): curvature = lax.psum(local_curv, ('coil', 'slab'))  101 us
    all_gather x2, blocking collectives, shards(): lax.all_gather(direction, 'coil', axis=1, tiled=True)[None]  75.4 us
    all_to_all x1, blocking collectives, shards(): lax.all_to_all(spread, 'slab', split_axis=2, concat_axis=1, tiled=True)  49.7 us
    all_to_all x1, blocking collectives, shards(): lax.all_to_all(returned, 'slab', split_axis=1, concat_axis=2, tiled=True)  34.2 us
    concatenate x12, local copies, waits for them, and re-layouts, convolve(): patches = jnp.concatenate(tap_list, axis=-1).reshape(-1, width_taps)  26.8 us
    all_to_all x1, waiting for transfers between devices, shards(): lax.all_to_all(spread, 'slab', split_axis=2, concat_axis=1, tiled=True)  26.5 us
  transfers between devices with their start and end apart: 16, of which 13 were waited for; matrix products, arithmetic and copies ran while one was open for 1% of the time, Pallas kernels for 0%

commit v1 on v0

v1 whole, which is shorter than its diff:
```python
import functools

import jax
import jax.numpy as jnp
import numpy as np
from jax import lax
from jax.experimental import pallas as pl
from jax.experimental.pallas import tpu as pltpu
from jax.sharding import PartitionSpec as P

F32 = jnp.float32
BF16 = jnp.bfloat16
REG = 0.5
ACROSS = 4
TRIM = True


def dft_parts(out_len, in_len, length):
    phases = (np.arange(out_len)[:, None] * np.arange(in_len)[None, :] % length) * (2.0 * np.pi / length)
    return np.cos(phases), np.sin(phases)


def in_bf16(table, parts=1):
    rest, out = table, []
    for _ in range(parts):
        part = rest.astype(np.float32).astype(jnp.bfloat16)
        out.append(part)
        rest = rest - part.astype(np.float64)
    return jnp.asarray(np.stack(out))


def make_tables(slabs, halves, rows, padded, side, grid):
    cos_p, sin_p = dft_parts(grid, side, grid)
    cells = slabs * halves * padded
    keep = np.arange(cells) % padded < rows
    cos_x = np.zeros((grid, cells))
    sin_x = np.zeros((grid, cells))
    cos_x[:, keep] = cos_p
    sin_x[:, keep] = sin_p
    return [
        in_bf16(np.stack([cos_x.T, sin_x.T]), 2),
        in_bf16(np.concatenate([cos_p, sin_p], axis=1), 2),
    ]


def cg_kernel(
    dims,
    adj_ref, den_ref, sens_hbm, kern_hbm, invr_hbm, invl_hbm, cin_hbm, cmid_hbm, cout_hbm,
    both_ref,
    adj_v, den_v, sens_v, kern_v, invr_v, invl_v, cin_v, cmid_v, cout_v,
    depth_t, fwdl_t, fwdr_t, invr_t, invl_t,
    b_own, b_send, b_all, b_far, b_near, b_halo, s_send, s_all, k_all, s_rr, s_ii,
    p_send, p_all, a_send, a_all, c_send, c_all, q_send, q_all, r_send, r_all, d_send, d_all, kf_keep,
    g_send, g_own, r_own_v, r_near, r_halo, n_send, n_sum, n_all, n_tot,
    first_w, mid_w, last_w, taps, taps_t, from_b, from_r, hidden,
    load_sem, send_sem, recv_sem,
):
    coils, slabs, halves, rows, padded, side, grid, feats, total = dims
    width = 2 * side
    cells = slabs * padded * halves
    c = lax.axis_index("coil")
    j = lax.axis_index("slab")
    home = c // halves
    across = ACROSS
    line = coils // across
    my_x = c // line
    my_y = lax.rem(c, line)
    lane = lax.broadcasted_iota(jnp.int32, (cells, width), 1)
    low = lane < side
    row_in_chunk = lax.rem(lax.broadcasted_iota(jnp.int32, (cells, width), 0), padded)
    barrier = pltpu.get_barrier_semaphore()
    native_coil = halves * j + lax.rem(c, halves)
    native_slab = c // halves

    def hello(coil, slab):
        pl.semaphore_signal(barrier, inc=1, device_id=to(coil, slab), device_id_type=pl.DeviceIdType.MESH)

    def to(coil, slab):
        return {"coil": coil, "slab": slab}

    def repeat(first, last, body):
        def step(k, carry):
            body(k)
            return carry

        lax.fori_loop(first, last, step, 0)

    loads = (
        (adj_ref, adj_v), (den_ref, den_v), (sens_hbm.at[0, 0], sens_v), (kern_hbm, kern_v),
        (invl_hbm, invl_v), (invr_hbm, invr_v), (cin_hbm, cin_v), (cmid_hbm, cmid_v), (cout_hbm, cout_v),
    )
    for index, (src, dst) in enumerate(loads):
        pltpu.make_async_copy(src, dst, load_sem.at[index]).start()

    def loaded(index):
        src, dst = loads[index]
        pltpu.make_async_copy(src, dst, load_sem.at[index]).wait()

    repeat(1, slabs, lambda k: hello(c, lax.rem(j + k, slabs)))
    repeat(1, coils, lambda k: hello(lax.rem(c + k, coils), j))

    def trim(ref):
        return ref.at[..., 0:rows, :] if TRIM else ref

    def tidy(values):
        return jnp.where(row_in_chunk < rows, values, 0.0) if TRIM else values

    def swap(values):
        return pltpu.roll(values, side, 1)

    def turn(values):
        rolled = swap(values)
        return jnp.where(low, -rolled, rolled)

    def remote(src, dst, phase, coil, slab):
        return pltpu.make_async_remote_copy(
            src_ref=src,
            dst_ref=dst,
            send_sem=send_sem.at[phase],
            recv_sem=recv_sem.at[phase],
            device_id=to(coil, slab),
            device_id_type=pl.DeviceIdType.MESH,
        )

    def took(ref, phase):
        pltpu.make_async_copy(ref, ref, recv_sem.at[phase]).wait()

    def sent(ref, phase):
        pltpu.make_async_copy(ref, ref, send_sem.at[phase]).wait()

    def to_slabs(src, dst, phase, short=False):
        view = trim if short else lambda ref: ref

        def step(k):
            other = lax.rem(j + k, slabs)
            remote(view(src.at[other]), view(dst.at[j]), phase, c, other).start()

        repeat(1, slabs, step)

    def to_coils(pick, dst, phase):
        def step(k, carry):
            other = lax.rem(c + k, coils)
            remote(pick(other), dst, phase, other, j).start()
            return carry

        lax.fori_loop(1, coils, step, 0)

    def to_beside(src, dst, phase, values=None):
        if values is not None:
            src[...] = values
        remote(src, dst.at[0], phase, lax.rem(c + 1, coils), j).start()
        remote(src, dst.at[1], phase, lax.rem(c + coils - 1, coils), j).start()
        dst[2] = src[...]

    def to_planes(src, dst, phase):
        def step(k):
            remote(src, dst.at[k], phase, c, lax.rem(j + 3 - k + slabs, slabs)).start()

        repeat(0, 3, step)
        repeat(4, 7, step)
        dst[3] = src[...]

    loaded(0)
    loaded(1)
    right = adj_v[:, 0, :] + REG * den_v[:, 0, :]
    b_own[...] = jnp.zeros_like(b_own)
    b_own[0:rows] = right
    b_send[...] = b_own[...].astype(BF16)
    b_all[0] = jnp.zeros_like(b_send)
    b_all[coils + 1] = jnp.zeros_like(b_send)
    b_all[c + 1] = b_send[...]

    pl.semaphore_wait(barrier, (slabs - 1) + (coils - 1))

    to_coils(lambda other: trim(b_send), trim(b_all.at[c + 1]), 0)
    to_beside(b_own, b_near, 16)

    far_row = j // across
    near_row = lax.rem(j, across)
    mine = near_row == my_x
    loaded(3)

    @pl.when(mine)
    def _():
        def share(k):
            other = lax.rem(j + k, slabs)
            remote(kern_v.at[other], k_all.at[far_row, near_row], 2, c, other).start()

        repeat(1, slabs, share)
        k_all[far_row, near_row] = kern_v[j]

    loaded(2)
    for block in range(slabs):
        for half in range(halves):
            first = (block * halves + half) * rows
            piece = sens_v[first : first + rows, :]
            piece = jnp.concatenate([piece, jnp.zeros((padded - rows, width), F32)], axis=0)
            s_send[block, half] = piece.astype(BF16)
            s_rr[first // rows * padded : (first // rows + 1) * padded] = piece
    to_slabs(s_send, s_all, 1, True)
    s_all[j] = s_send[j]
    maps = s_rr[...]
    rolled = swap(maps)
    s_rr[...] = jnp.where(low, maps, rolled)
    s_ii[...] = jnp.where(low, -rolled, maps)

    square = slabs * halves * padded
    row = lax.broadcasted_iota(jnp.int32, (square, square), 0)
    col = lax.broadcasted_iota(jnp.int32, (square, square), 1)
    group = halves * padded
    turns = lax.rem((row // group) * (col // group), slabs)
    same = (lax.rem(row, group) == lax.rem(col, group)) & (lax.rem(row, padded) < rows)
    turns = jnp.where(same, turns, slabs)
    for part, values in enumerate(dft_parts(slabs, 2, slabs)):
        table = jnp.zeros((square, square), F32)
        for index in range(slabs):
            table = jnp.where(turns == index, float(values[index, 1]), table)
        high = table.astype(BF16)
        depth_t[0, part * square : (part + 1) * square] = high
        depth_t[1, part * square : (part + 1) * square] = (table - high.astype(F32)).astype(BF16)
    loaded(4)
    for part in range(2):
        top = invl_v[part].astype(F32)
        turned = pltpu.roll(top, side, 1)
        left = lax.broadcasted_iota(jnp.int32, top.shape, 1) < side
        invl_t[part, 0:grid] = invl_v[part]
        invl_t[part, grid:] = jnp.where(left, -turned, turned).astype(BF16)
    flipped = jnp.transpose(invl_v[0].astype(F32)).astype(BF16)
    fwdl_t[:, 0:grid] = flipped
    fwdl_t[0:side, grid:] = -flipped[side:]
    fwdl_t[side:, grid:] = flipped[:side]
    loaded(5)
    cosines = jnp.transpose(invr_v[0, 0].astype(F32)).astype(BF16)
    sines = jnp.transpose(invr_v[0, 1].astype(F32)).astype(BF16)
    fwdr_t[0:grid, 0:cells] = cosines
    fwdr_t[0:grid, cells:] = sines
    fwdr_t[grid:, 0:cells] = -sines
    fwdr_t[grid:, cells:] = cosines
    for part in range(2):
        invr_t[part, 0:cells, 0:grid] = invr_v[part, 0]
        invr_t[part, 0:cells, grid:] = -invr_v[part, 1]
        invr_t[part, cells:, 0:grid] = invr_v[part, 1]
        invr_t[part, cells:, grid:] = invr_v[part, 0]

    def depth_dft(image):
        both = jnp.dot(depth_t[0], image, preferred_element_type=F32)
        both = both + jnp.dot(depth_t[1], image, preferred_element_type=F32)
        return both[:cells], turn(both[cells:])

    def coil_images(field):
        field = tidy(field)
        product = s_rr[...] * field + s_ii[...] * swap(field)
        return product.astype(BF16)

    def to_depth(product):
        real, imag = depth_dft(product)
        return (real - imag).astype(BF16).reshape(slabs, halves, padded, width)

    def spectrum(image_ref):
        image = tidy(image_ref[...].astype(F32).reshape(cells, width)).astype(BF16)
        lines = jnp.dot(image, fwdl_t[...], preferred_element_type=F32).astype(BF16)
        stacked = jnp.concatenate([lines[:, :grid], lines[:, grid:]], axis=0)
        return jnp.dot(fwdr_t[...], stacked, preferred_element_type=F32)

    took(trim(b_all.at[0 : coils - 1]), 0)
    product = coil_images(b_all[1 : coils + 1].astype(F32).reshape(cells, width))
    p_send[...] = product.astype(F32).reshape(slabs, halves, padded, width).astype(BF16)
    to_slabs(p_send, p_all, 13, True)
    p_all[j] = p_send[j]
    prior_weights(dims, loaded, cin_v, cmid_v, cout_v, first_w, mid_w, last_w)

    half_here = lax.rem(c, halves)

    @pl.when(j == home)
    def _():
        def share(k):
            other = lax.rem(j + k, slabs)
            remote(b_all.at[1 + halves * other + half_here], b_far, 5, c, other).start()

        repeat(1, slabs, share)
        b_far[...] = b_all[1 + halves * j + half_here]

    @pl.when(mine)
    def _():
        took(k_all.at[0, 0 : across - 1], 2)

    @pl.when(jnp.logical_not(mine))
    def _():
        took(k_all.at[0], 2)

    def pass_on(k):
        other = lax.rem(my_x + k, across)
        remote(k_all.at[:, my_x], k_all.at[:, my_x], 15, other * line + my_y, j).start()

    repeat(1, across, pass_on)

    took(trim(p_all.at[0 : slabs - 1]), 13)
    a_send[...] = to_depth(tidy(p_all[...].astype(F32).reshape(cells, width)).astype(BF16))
    to_slabs(a_send, a_all, 4, True)
    a_all[j] = a_send[j]
    took(trim(s_all.at[0 : slabs - 1]), 1)
    maps = tidy(s_all[...].astype(F32).reshape(cells, width))
    rolled = swap(maps)
    s_rr[...] = jnp.where(low, maps, rolled)
    s_ii[...] = jnp.where(low, -rolled, maps)
    took(trim(a_all.at[0 : slabs - 1]), 4)
    took(k_all.at[:, 0 : across - 1], 15)
    weight = k_all[...].reshape(grid, grid)
    freq = spectrum(a_all)
    kf_keep[0:grid] = weight * freq[:grid]
    kf_keep[grid:] = weight * freq[grid:]
    energy = jnp.sum(kf_keep[...] * freq)

    sub = lax.broadcasted_iota(jnp.int32, (8, 128), 0)

    def message(values):
        packed = jnp.zeros((8, 128), F32)
        for index, value in enumerate(values):
            packed = jnp.where(sub == index, value, packed)
        return packed

    third = lax.broadcasted_iota(jnp.int32, (1, width), 1) // (width // 3)

    def as_parts(value):
        value = jnp.broadcast_to(value, (1, width))
        high = value.astype(BF16).astype(F32)
        mid = (value - high).astype(BF16).astype(F32)
        return jnp.where(third == 0, high, jnp.where(third == 1, mid, value - high - mid))

    def with_sums(values, first_sum, second_sum):
        values = jnp.where(row_in_chunk == rows, as_parts(first_sum), values)
        return jnp.where(row_in_chunk == rows + 1, as_parts(second_sum), values)

    def from_parts(line):
        size = width // 3
        joined = line[:, 0:size] + line[:, size : 2 * size] + line[:, 2 * size :]
        return joined[:, 0:1]

    def sum_slabs(src, dst, phase):
        def step(k, carry):
            other = lax.rem(j + k, slabs)
            remote(src, dst.at[j], phase, c, other).start()
            return carry

        lax.fori_loop(1, slabs, step, 0)
        dst[j] = src[...]

    scaled = kf_keep[...].astype(BF16)
    back = jnp.dot(invr_t[0], scaled, preferred_element_type=F32)
    back = (back + jnp.dot(invr_t[1], scaled, preferred_element_type=F32)).astype(BF16)
    back = jnp.concatenate([back[:cells], back[cells:]], axis=1)
    image = jnp.dot(back, invl_t[0], preferred_element_type=F32)
    image = (image + jnp.dot(back, invl_t[1], preferred_element_type=F32)) * (1.0 / total)
    bb_part = jnp.sum(right * right)
    image = with_sums(image, energy * (1.0 / total), bb_part)
    c_send[...] = image.astype(BF16).reshape(slabs, halves, padded, width)
    to_slabs(c_send, c_all, 6)
    c_all[j] = c_send[j]
    took(c_all.at[0 : slabs - 1], 6)
    sums = jnp.sum(c_all[:, 0].astype(F32), axis=0)
    energy_sum = from_parts(sums[rows : rows + 1])
    bb_sum = from_parts(sums[rows + 1 : rows + 2])
    image = c_all[...].astype(F32).reshape(cells, width)
    image = jnp.where(row_in_chunk < rows, image, 0.0).astype(BF16)
    real, imag = depth_dft(image)
    image = real + imag
    coil_part = s_rr[...] * image - s_ii[...] * swap(image)
    q_send[...] = with_sums(coil_part, energy_sum, bb_sum).astype(BF16).reshape(coils, padded, width)
    to_coils(lambda other: q_send.at[other], q_all.at[c], 8)
    q_all[c] = q_send[c]

    took(b_near.at[0:2], 16)
    to_planes(b_near, b_halo, 3)

    @pl.when(j != home)
    def _():
        took(b_far, 5)

    chunk_row = lax.broadcasted_iota(jnp.int32, (padded, width), 0)
    b_here = jnp.where(chunk_row < rows, b_far[...].astype(F32), 0.0)
    took(q_all.at[0 : coils - 1], 8)
    sums = jnp.sum(q_all[...].astype(F32), axis=0)
    g_coils = jnp.where(chunk_row < rows, sums, 0.0)
    g_send[...] = g_coils
    g_here = g_coils + REG * b_here
    energy0 = from_parts(sums[rows : rows + 1])
    bb = from_parts(sums[rows + 1 : rows + 2])
    alpha0 = bb / (energy0 + REG * bb)
    resid = b_here - alpha0 * g_here
    r_send[...] = resid.astype(BF16)
    to_coils(lambda other: trim(r_send), trim(r_all.at[c]), 9)
    r_all[c] = r_send[...]

    @pl.when(j == home)
    def _():
        pltpu.make_async_copy(g_send, g_own, recv_sem.at[10]).start()

    @pl.when(j != home)
    def _():
        remote(g_send, g_own, 10, native_coil, native_slab).start()

    rr_part = jnp.sum(resid * resid)
    rb_part = jnp.sum(resid * b_here)

    took(b_halo.at[0:6], 3)
    prior_taps(dims, c, j, b_halo[...], taps, taps_t)
    prior_sums(dims, 0, taps_t, first_w, from_b)

    took(trim(r_all.at[0 : coils - 1]), 9)
    d_send[...] = to_depth(coil_images(r_all[...].astype(F32).reshape(cells, width)))
    to_slabs(d_send, d_all, 11, True)
    d_all[j] = d_send[j]
    took(g_own, 10)
    r_own = b_own[...] - alpha0 * (g_own[...] + REG * b_own[...])
    to_beside(r_own_v, r_near, 17, r_own)
    prior_sums(dims, 1, taps_t, first_w, from_b)
    took(r_near.at[0:2], 17)
    to_planes(r_near, r_halo, 12)

    took(trim(d_all.at[0 : slabs - 1]), 11)
    freq = spectrum(d_all)
    cross = jnp.sum(kf_keep[...] * freq)
    power = freq * freq
    energy = jnp.sum(weight * (power[:grid] + power[grid:]))
    n_send[...] = message([energy * (1.0 / total), cross * (1.0 / total), rr_part, rb_part])
    sum_slabs(n_send, n_all, 7)
    took(r_halo.at[0:6], 12)
    prior_taps(dims, c, j, r_halo[...], taps, taps_t)
    prior_sums(dims, 0, taps_t, first_w, from_r)
    took(n_all.at[0 : slabs - 1], 7)
    n_sum[...] = jnp.sum(n_all[...], axis=0)
    to_coils(lambda other: n_sum, n_tot.at[c], 14)
    n_tot[c] = n_sum[...]
    prior_sums(dims, 1, taps_t, first_w, from_r)

    took(n_tot.at[0 : coils - 1], 14)
    sums = jnp.sum(n_tot[...], axis=0)
    energy1 = sums[0:1, 0:1]
    cross1 = sums[1:2, 0:1]
    rr = sums[2:3, 0:1]
    rb = sums[3:4, 0:1]
    beta = rr / bb
    curvature = energy1 + 2.0 * beta * cross1 + beta * beta * energy0
    curvature = curvature + REG * (rr + 2.0 * beta * rb + beta * beta * bb)
    alpha1 = rr / curvature
    for_b = alpha0 + alpha1 * beta
    solved = (for_b * b_own[...] + alpha1 * r_own)[0:rows]
    for r in range(rows):
        both_ref[r] = solved[r : r + 1]
    prior_rest(dims, c, j, for_b, alpha1, from_b, from_r, hidden, mid_w, last_w, solved, both_ref.at[pl.ds(rows, rows)])

    @pl.when(j != home)
    def _():
        sent(g_send, 10)

    @pl.when(j == home)
    def _():
        sent(b_all.at[0 : slabs - 1], 5)

    @pl.when(mine)
    def _():
        sent(kern_v.at[0 : slabs - 1], 2)

    sent(trim(b_all.at[0 : coils - 1]), 0)
    sent(trim(s_all.at[0 : slabs - 1]), 1)
    sent(b_halo.at[0:6], 3)
    sent(b_near.at[0:2], 16)
    sent(trim(a_all.at[0 : slabs - 1]), 4)
    sent(c_all.at[0 : slabs - 1], 6)
    sent(n_all.at[0 : slabs - 1], 7)
    sent(q_all.at[0 : coils - 1], 8)
    sent(trim(r_all.at[0 : coils - 1]), 9)
    sent(trim(d_all.at[0 : slabs - 1]), 11)
    sent(r_halo.at[0:6], 12)
    sent(r_near.at[0:2], 17)
    sent(trim(p_all.at[0 : slabs - 1]), 13)
    sent(n_tot.at[0 : coils - 1], 14)
    sent(k_all.at[:, 0 : across - 1], 15)


def prior_weights(dims, loaded, cin_v, cmid_v, cout_v, first_w, mid_w, last_w):
    coils, slabs, halves, rows, padded, side, grid, feats, total = dims
    strip = 3 * padded
    deep = rows + 4
    loaded(6)
    tap_shape = (54, 18 * strip)
    tap = lax.broadcasted_iota(jnp.int32, tap_shape, 0)
    at = lax.broadcasted_iota(jnp.int32, tap_shape, 1)
    kind = at // strip
    place = lax.rem(at, strip)
    inner = lax.rem(place, padded)
    image_row = (place // padded) * rows + inner
    rest = tap - (kind // 6) * 18 - lax.rem(kind, 6)
    for r in range(deep):
        dx = image_row - (r + 3)
        hit = (rest == dx * 6) & (dx >= 0) & (dx < 3) & (inner < rows)
        pick = jnp.where(hit, 1.0, 0.0).astype(BF16)
        part = lax.dot_general(cin_v[...], pick, (((0,), (0,)), ((), ())), preferred_element_type=F32).astype(BF16)
        first_w[2 * r * feats : (2 * r + 1) * feats] = part
        if r > 0:
            first_w[(2 * r - 1) * feats : 2 * r * feats] = part
    first_w[(2 * deep - 1) * feats :] = jnp.zeros((feats, 18 * strip), BF16)
    loaded(7)
    mid_w[...] = jnp.zeros_like(mid_w)
    loaded(8)
    last_w[...] = jnp.zeros_like(last_w)
    for dz in range(3):
        for dx in range(3):
            for dy in range(3):
                first = ((dz * 3 + dx) * 3 + dy) * feats
                block = cmid_v[:, first : first + feats]
                for place in ((0,), (2, 3), (1,))[dy]:
                    mid_w[dz, place * feats : (place + 1) * feats, dx * feats : (dx + 1) * feats] = block
                last_w[dz, dy * 2 : dy * 2 + 2, dx * feats : (dx + 1) * feats] = cout_v[:, first : first + feats]


def shift_lanes(values, up):
    at = lax.broadcasted_iota(jnp.int32, values.shape, 1)
    count = values.shape[1]
    if up:
        return jnp.where(at == 0, 0.0, pltpu.roll(values, 1, 1))
    return jnp.where(at == count - 1, 0.0, pltpu.roll(values, count - 1, 1))


def prior_taps(dims, c, j, field, taps, taps_t):
    coils, slabs, halves, rows, padded, side, grid, feats, total = dims
    strip = 3 * padded
    width = 2 * side
    field = jnp.stack([field[:, k] for k in (0, 2, 1)], axis=1).reshape(21, padded, width)
    index = lax.broadcasted_iota(jnp.int32, (21, padded, width), 0)
    plane = j + index // 3 - 3
    chunk = c + lax.rem(index, 3) - 1
    inside = (plane >= 0) & (plane < slabs) & (chunk >= 0) & (chunk < coils)
    inside = inside & (lax.broadcasted_iota(jnp.int32, (21, padded, width), 1) < rows)
    field = jnp.where(inside, field, 0.0).reshape(7 * strip, width)
    for part in range(2):
        values = field[:, part * side : (part + 1) * side]
        for dy, shifted in enumerate((shift_lanes(values, True), values, shift_lanes(values, False))):
            taps[:, dy * 2 + part] = shifted.reshape(7, strip, side)
    for p in range(5):
        part = jnp.transpose(taps[p : p + 3].reshape(3 * 6 * strip, side))
        high = part.astype(BF16)
        taps_t[0, p] = high
        taps_t[1, p] = (part - high.astype(F32)).astype(BF16)


def prior_sums(dims, turn, taps_t, first_w, result):
    coils, slabs, halves, rows, padded, side, grid, feats, total = dims
    first, last = ((0, 2), (2, 5))[turn]
    inner = 18 * 3 * padded
    contract = (((1,), (1,)), ((), ()))
    tall = (last - first) * side
    high = taps_t[0, first:last].reshape(tall, inner)
    low = taps_t[1, first:last].reshape(tall, inner)
    sums = lax.dot_general(high, first_w[...], contract, preferred_element_type=F32)
    sums = sums + lax.dot_general(low, first_w[...], contract, preferred_element_type=F32)
    result[first:last] = sums.reshape(last - first, side, sums.shape[1])


def prior_rest(dims, c, j, for_b, for_r, from_b, from_r, hidden, mid_w, last_w, solved, out_ref):
    coils, slabs, halves, rows, padded, side, grid, feats, total = dims
    width = 2 * side
    pair = 2 * feats
    deep = rows + 4
    deep_lane = lax.broadcasted_iota(jnp.int32, (1, deep * pair), 1)
    out_row = deep_lane // pair + lax.rem(deep_lane, pair) // feats
    at_row = c * rows - 2 + out_row
    row_ok = (at_row >= 0) & (at_row < side) & (out_row < deep)
    for p in range(5):
        at_plane = j + p - 2
        ok = row_ok & (at_plane >= 0) & (at_plane < slabs)
        scale_b = jnp.where(ok, for_b, 0.0)
        scale_r = jnp.where(ok, for_r, 0.0)
        for r in range(deep):
            span = slice(r * pair, (r + 1) * pair)
            feat = from_b[p, :, span] * scale_b[:, span] + from_r[p, :, span] * scale_r[:, span]
            hidden[p, r] = jnp.maximum(feat, 0.0).astype(BF16)
    wide = rows + 2
    cell = lax.broadcasted_iota(jnp.int32, (side, pair), 0)
    left = lax.broadcasted_iota(jnp.int32, (side, pair), 1) < feats
    result = None
    for p in range(3):
        feat = None
        for dz in range(3):
            data = jnp.concatenate(
                [
                    hidden[p + dz, 0:wide].reshape(wide * side, pair),
                    hidden[p + dz, 2 : wide + 2].reshape(wide * side, pair),
                ],
                axis=1,
            )
            piece = lax.dot_general(data, mid_w[dz], (((1,), (1,)), ((), ())), preferred_element_type=F32)
            feat = piece if feat is None else feat + piece
        at_plane = j + p - 1
        plane_ok = (at_plane >= 0) & (at_plane < slabs)
        maps = []
        for r in range(wide):
            sides = feat[r * side : (r + 1) * side, :pair]
            centre = feat[r * side : (r + 1) * side, pair:]
            ahead = jnp.where(cell == 0, 0.0, pltpu.roll(sides, 1, 0))
            behind = jnp.where(cell == side - 1, 0.0, pltpu.roll(sides, side - 1, 0))
            sides = jnp.where(left, ahead, behind)
            value = jnp.maximum(sides + pltpu.roll(sides, feats, 1) + centre, 0.0)
            at_row = c * rows - 1 + r
            ok = plane_ok & (at_row >= 0) & (at_row < side)
            maps.append(jnp.where(ok, value, 0.0).astype(BF16))
        pairs = [jnp.where(left, maps[r], maps[r + 1]) for r in range(wide - 1)]
        pairs.append(maps[wide - 1])
        data = jnp.concatenate(
            [jnp.concatenate(pairs[0:rows], axis=0), jnp.concatenate(pairs[2 : rows + 2], axis=0)], axis=1
        )
        piece = lax.dot_general(last_w[p], data, (((1,), (1,)), ((), ())), preferred_element_type=F32)
        result = piece if result is None else result + piece
    for r in range(rows):
        span = result[:, r * side : (r + 1) * side]
        value = shift_lanes(span, True)[0:2] + span[2:4] + shift_lanes(span, False)[4:6]
        out_ref[r, :, 0:side] = solved[r : r + 1, 0:side] + value[0:1]
        out_ref[r, :, side:width] = solved[r : r + 1, side:width] + value[1:2]


def shards(adjoint_data, denoised, sensitivity, kernel, conv_in, conv_mid, conv_out):
    coils = lax.axis_size("coil")
    slabs = lax.axis_size("slab")
    rows = adjoint_data.shape[1]
    width = adjoint_data.shape[2]
    side = sensitivity.shape[2]
    grid = kernel.shape[2]
    feats = conv_mid.shape[1]
    halves = coils // slabs
    padded = 8
    deep = rows + 4
    total = float(slabs * grid * grid)
    dims = (coils, slabs, halves, rows, padded, side, grid, feats, total)
    tables = make_tables(slabs, halves, rows, padded, side, grid)
    cells = slabs * halves * padded
    kx = kernel.shape[1]
    layers = (conv_in, conv_mid.T, conv_out.T)
    vmem = pltpu.VMEM
    block = (slabs, halves, padded, width)
    strip = 3 * padded
    scratch = [
        vmem((rows, 1, width), F32), vmem((rows, 1, width), F32), vmem((side, width), F32), vmem((slabs, kx, grid), F32),
        *[vmem(t.shape, BF16) for t in (*tables, *layers)],
        vmem((2, 2 * cells, cells), BF16), vmem((2 * side, 2 * grid), BF16), vmem((2 * grid, 2 * cells), BF16),
        vmem((2, 2 * cells, 2 * grid), BF16), vmem((2, 2 * grid, 2 * side), BF16),
        vmem((padded, width), F32), vmem((padded, width), BF16), vmem((coils + 2, padded, width), BF16),
        vmem((padded, width), BF16), vmem((3, padded, width), F32), vmem((7, 3, padded, width), F32),
        vmem(block, BF16), vmem(block, BF16),
        vmem((slabs // ACROSS, ACROSS, kx, grid), F32),
        vmem((cells, width), F32), vmem((cells, width), F32),
        *[vmem(block, BF16)] * 6,
        vmem((coils, padded, width), BF16), vmem((coils, padded, width), BF16),
        vmem((padded, width), BF16), vmem((coils, padded, width), BF16),
        vmem(block, BF16), vmem(block, BF16),
        vmem((2 * grid, grid), F32),
        vmem((padded, width), F32), vmem((padded, width), F32),
        vmem((padded, width), F32), vmem((3, padded, width), F32), vmem((7, 3, padded, width), F32),
        vmem((8, 128), F32), vmem((8, 128), F32), vmem((slabs, 8, 128), F32), vmem((coils, 8, 128), F32),
        vmem((2 * deep * feats, 18 * strip), BF16), vmem((3, 4 * feats, 4 * feats), BF16), vmem((3, 8, 4 * feats), BF16),
        vmem((7, 6, strip, side), F32), vmem((2, 5, side, 18 * strip), BF16),
        vmem((5, side, 2 * deep * feats), F32), vmem((5, side, 2 * deep * feats), F32),
        vmem((5, deep, side, 2 * feats), BF16),
        pltpu.SemaphoreType.DMA((9,)), pltpu.SemaphoreType.DMA((18,)), pltpu.SemaphoreType.DMA((18,)),
    ]
    near = pl.BlockSpec(memory_space=pltpu.VMEM)
    far = pl.BlockSpec(memory_space=pltpu.HBM)
    shape = jax.ShapeDtypeStruct((2 * rows, 1, width), F32)
    both = pl.pallas_call(
        functools.partial(cg_kernel, dims),
        out_shape=shape,
        in_specs=[far] * 9,
        out_specs=near,
        scratch_shapes=scratch,
        compiler_params=pltpu.CompilerParams(has_side_effects=True, collective_id=0, vmem_limit_bytes=60 << 20),
        name="cg",
    )(adjoint_data.transpose(1, 0, 2), denoised.transpose(1, 0, 2), sensitivity, kernel, *tables, *layers)
    return (both[:rows].transpose(1, 0, 2), both[rows:].transpose(1, 0, 2))


def solution(mesh):
    placed = (
        P("slab", "coil", None),
        P("slab", "coil", None),
        P("coil", "slab", None, None),
        P(None, "slab", None),
        P(),
        P(),
        P(),
    )
    return jax.shard_map(
        shards,
        mesh=mesh,
        in_specs=placed,
        out_specs=(P("slab", "coil", None), P("slab", "coil", None)),
        check_vma=False,
    )
```

time: 1030 us -> 89.6 us (0.09)
  blocking collectives: 455 us -> 0 us
  waiting for transfers between devices: 359 us -> 0 us
  Pallas kernels: 0 us -> 87.4 us
  local copies, waits for them, and re-layouts: 64.6 us -> 1.33 us
  starting transfers between devices: 63.1 us -> 0 us
  matrix products: 52.4 us -> 0 us
  between operations: 19.8 us -> 0.64 us
  other arithmetic: 12 us -> 0 us
    psum x3 -> x0, blocking collectives: 296 us -> none  [the longest x2 195 us: total_squares(): return lax.psum(jnp.sum(residual * residual), ('coil', 'slab'))]
    unnamed x4 -> x0, waiting for transfers between devices: 290 us -> none
    pallas_call x0 -> x1, Pallas kernels: none -> 87.4 us  [shards(): pl.pallas_call(functools.partial(cg_kernel, dims), out_shape=shape, in_sp...]
    all_to_all x2 -> x0, blocking collectives: 83.8 us -> none  [the longest x1 49.7 us: shards(): lax.all_to_all(spread, 'slab', split_axis=2, concat_axis=1, tiled=True)]
    all_gather x2 -> x0, blocking collectives: 75.4 us -> none  [shards(): lax.all_gather(direction, 'coil', axis=1, tiled=True)[None]]
    all_to_all x2 -> x0, waiting for transfers between devices: 53 us -> none  [the longest x1 26.5 us: shards(): lax.all_to_all(spread, 'slab', split_axis=2, concat_axis=1, tiled=True)]
    dot_general x29 -> x0, matrix products: 52.4 us -> none  [the longest x8 18 us: along_axis(): imag_part = jnp.einsum(einsum_form, tables[1], values, precision=highest)]
    ppermute x12 -> x0, starting transfers between devices: 35.4 us -> none  [the longest x6 22.1 us: with_halo(): lax.ppermute(tail, axis, [(i, (i + 1) % count) for i in range(ends)])]
  transfers between devices with their start and end apart: 16 -> 0, of which waited for: 13 -> 0; matrix products, arithmetic and copies ran while one was open for 1% -> 0% of each run, Pallas kernels for 0% -> 0%
where the time goes in v1:
time: 89.6 us; the launch traced here: 89.4 us
  Pallas kernels  87.4 us (98%)
  local copies, waits for them, and re-layouts  1.33 us (1%)
    pallas_call x1, Pallas kernels, shards(): pl.pallas_call(functools.partial(cg_kernel, dims), out_shape=shape, in_sp...  87.4 us

profile of v1, /device:TPU:1, one launch (start us, length us, event | category | flops | bytes accessed | tf_op | source)
XLA Modules:
  0.0 89.4 jit_solution(8808363203747289689)
XLA Ops:
  0.6 87.4 %cg.1 = f32[12,1,384]{2,1,0:T(1,128)} custom-call(f32[6,1,384]{2,1,0:T(1,128)} %bitcast.9, f32[6,1,384]{2,1,0:T(1,128)} %bitcast.10, f32[1,1,192,384]{3,2,1,0:T(8,128)} %sens_hbm.1, f32[16,24,384]{2,1,0:T(8,128)} %kern_hbm.1, bf16[2,2,256,384]{3,2,1,0:T(8,128)(2,1)} %constant.4.clone.invr_hbm, bf16[2,384,384]{2,1,0:T(8,128)(2,1)} %constant.5.clone.invl_hbm, ...), custom_call_target="tpu_custom_call" | custom-call | tf_op jit(solution)/shard_map/cg/pallas_call | solution.py:668
  88.1 1.3 %slice_bitcast_fusion = (f32[1,6,384]{2,0,1:T(1,128)}, f32[1,6,384]{2,0,1:T(1,128)}) fusion(f32[12,1,384]{2,1,0:T(1,128)} %cg.1), kind=kLoop, calls=%fused_computation | loop fusion | bytes 36864 | tf_op jit(solution)/shard_map/transpose | solution.py:677

commit v2 on v1

--- a/solution.py
+++ b/solution.py
@@ -85,6 +85,17 @@
 
         lax.fori_loop(first, last, step, 0)
 
+    def far_first(index, count):
+        step = (index + 1) // 2
+        return count // 2 + step - 2 * step * lax.rem(index, 2)
+
+    def slab_at(index):
+        return lax.rem(j + far_first(index, slabs), slabs)
+
+    def coil_at(index):
+        along = lax.rem(my_y + far_first(index // across, line), line)
+        return lax.rem(my_x + far_first(lax.rem(index, across), across), across) * line + along
+
     loads = (
         (adj_ref, adj_v), (den_ref, den_v), (sens_hbm.at[0, 0], sens_v), (kern_hbm, kern_v),
         (invl_hbm, invl_v), (invr_hbm, invr_v), (cin_hbm, cin_v), (cmid_hbm, cmid_v), (cout_hbm, cout_v),
@@ -96,8 +107,8 @@
         src, dst = loads[index]
         pltpu.make_async_copy(src, dst, load_sem.at[index]).wait()
 
-    repeat(1, slabs, lambda k: hello(c, lax.rem(j + k, slabs)))
-    repeat(1, coils, lambda k: hello(lax.rem(c + k, coils), j))
+    repeat(0, coils - 1, lambda k: hello(coil_at(k), j))
+    repeat(0, slabs - 1, lambda k: hello(c, slab_at(k)))
 
     def trim(ref):
         return ref.at[..., 0:rows, :] if TRIM else ref
@@ -132,18 +143,17 @@
         view = trim if short else lambda ref: ref
 
         def step(k):
-            other = lax.rem(j + k, slabs)
+            other = slab_at(k)
             remote(view(src.at[other]), view(dst.at[j]), phase, c, other).start()
 
-        repeat(1, slabs, step)
+        repeat(0, slabs - 1, step)
 
     def to_coils(pick, dst, phase):
-        def step(k, carry):
-            other = lax.rem(c + k, coils)
+        def step(k):
+            other = coil_at(k)
             remote(pick(other), dst, phase, other, j).start()
-            return carry
-
-        lax.fori_loop(1, coils, step, 0)
+
+        repeat(0, coils - 1, step)
 
     def to_beside(src, dst, phase, values=None):
         if values is not None:
@@ -311,12 +321,12 @@
     kf_keep[grid:] = weight * freq[grid:]
     energy = jnp.sum(kf_keep[...] * freq)
 
-    sub = lax.broadcasted_iota(jnp.int32, (8, 128), 0)
+    quarter = lax.broadcasted_iota(jnp.int32, (1, 128), 1) // 32
 
     def message(values):
-        packed = jnp.zeros((8, 128), F32)
+        packed = jnp.zeros((1, 128), F32)
         for index, value in enumerate(values):
-            packed = jnp.where(sub == index, value, packed)
+            packed = jnp.where(quarter == index, value, packed)
         return packed
 
     third = lax.broadcasted_iota(jnp.int32, (1, width), 1) // (width // 3)
@@ -337,12 +347,10 @@
         return joined[:, 0:1]
 
     def sum_slabs(src, dst, phase):
-        def step(k, carry):
-            other = lax.rem(j + k, slabs)
-            remote(src, dst.at[j], phase, c, other).start()
-            return carry
-
-        lax.fori_loop(1, slabs, step, 0)
+        def step(k):
+            remote(src, dst.at[j], phase, c, slab_at(k)).start()
+
+        repeat(0, slabs - 1, step)
         dst[j] = src[...]
 
     scaled = kf_keep[...].astype(BF16)
@@ -435,10 +443,10 @@
 
     took(n_tot.at[0 : coils - 1], 14)
     sums = jnp.sum(n_tot[...], axis=0)
-    energy1 = sums[0:1, 0:1]
-    cross1 = sums[1:2, 0:1]
-    rr = sums[2:3, 0:1]
-    rb = sums[3:4, 0:1]
+    energy1 = sums[:, 0:1]
+    cross1 = sums[:, 32:33]
+    rr = sums[:, 64:65]
+    rb = sums[:, 96:97]
     beta = rr / bb
     curvature = energy1 + 2.0 * beta * cross1 + beta * beta * energy0
     curvature = curvature + REG * (rr + 2.0 * beta * rb + beta * beta * bb)
@@ -655,7 +663,7 @@
         vmem((2 * grid, grid), F32),
         vmem((padded, width), F32), vmem((padded, width), F32),
         vmem((padded, width), F32), vmem((3, padded, width), F32), vmem((7, 3, padded, width), F32),
-        vmem((8, 128), F32), vmem((8, 128), F32), vmem((slabs, 8, 128), F32), vmem((coils, 8, 128), F32),
+        vmem((1, 128), F32), vmem((1, 128), F32), vmem((slabs, 1, 128), F32), vmem((coils, 1, 128), F32),
         vmem((2 * deep * feats, 18 * strip), BF16), vmem((3, 4 * feats, 4 * feats), BF16), vmem((3, 8, 4 * feats), BF16),
         vmem((7, 6, strip, side), F32), vmem((2, 5, side, 18 * strip), BF16),
         vmem((5, side, 2 * deep * feats), F32), vmem((5, side, 2 * deep * feats), F32),

time: 89.6 us -> 84.7 us (0.945)
  Pallas kernels: 87.4 us -> 82.5 us
    pallas_call x1, Pallas kernels: 87.4 us -> 82.5 us  [shards(): pl.pallas_call(functools.partial(cg_kernel, dims), out_shape=shape, in_sp...]
where the time goes in v2:
time: 84.7 us; the launch traced here: 84.5 us
  Pallas kernels  82.5 us (97%)
  local copies, waits for them, and re-layouts  1.33 us (2%)
    pallas_call x1, Pallas kernels, shards(): pl.pallas_call(functools.partial(cg_kernel, dims), out_shape=shape, in_sp...  82.5 us

profile of v2, /device:TPU:1, one launch (start us, length us, event | category | flops | bytes accessed | tf_op | source)
XLA Modules:
  0.0 84.5 jit_solution(3339152141917248461)
XLA Ops:
  0.6 82.5 %cg.1 = f32[12,1,384]{2,1,0:T(1,128)} custom-call(f32[6,1,384]{2,1,0:T(1,128)} %bitcast.9, f32[6,1,384]{2,1,0:T(1,128)} %bitcast.10, f32[1,1,192,384]{3,2,1,0:T(8,128)} %sens_hbm.1, f32[16,24,384]{2,1,0:T(8,128)} %kern_hbm.1, bf16[2,2,256,384]{3,2,1,0:T(8,128)(2,1)} %constant.4.clone.invr_hbm, bf16[2,384,384]{2,1,0:T(8,128)(2,1)} %constant.5.clone.invl_hbm, ...), custom_call_target="tpu_custom_call" | custom-call | tf_op jit(solution)/shard_map/cg/pallas_call | solution.py:676
  83.2 1.3 %slice_bitcast_fusion = (f32[1,6,384]{2,0,1:T(1,128)}, f32[1,6,384]{2,0,1:T(1,128)}) fusion(f32[12,1,384]{2,1,0:T(1,128)} %cg.1), kind=kLoop, calls=%fused_computation | loop fusion | bytes 36864 | tf_op jit(solution)/shard_map/transpose | solution.py:685

commit v3 on v2

--- a/solution.py
+++ b/solution.py
@@ -432,13 +432,13 @@
     energy = jnp.sum(weight * (power[:grid] + power[grid:]))
     n_send[...] = message([energy * (1.0 / total), cross * (1.0 / total), rr_part, rb_part])
     sum_slabs(n_send, n_all, 7)
-    took(r_halo.at[0:6], 12)
-    prior_taps(dims, c, j, r_halo[...], taps, taps_t)
-    prior_sums(dims, 0, taps_t, first_w, from_r)
     took(n_all.at[0 : slabs - 1], 7)
     n_sum[...] = jnp.sum(n_all[...], axis=0)
     to_coils(lambda other: n_sum, n_tot.at[c], 14)
     n_tot[c] = n_sum[...]
+    took(r_halo.at[0:6], 12)
+    prior_taps(dims, c, j, r_halo[...], taps, taps_t)
+    prior_sums(dims, 0, taps_t, first_w, from_r)
     prior_sums(dims, 1, taps_t, first_w, from_r)
 
     took(n_tot.at[0 : coils - 1], 14)

time: 84.7 us -> 84.6 us (level)
  no operation moved by 1% of the time
where the time goes in v3:
time: 84.6 us; the launch traced here: 84.5 us
  Pallas kernels  82.5 us (98%)
  local copies, waits for them, and re-layouts  1.33 us (2%)
    pallas_call x1, Pallas kernels, shards(): pl.pallas_call(functools.partial(cg_kernel, dims), out_shape=shape, in_sp...  82.5 us

profile of v3, /device:TPU:1, one launch (start us, length us, event | category | flops | bytes accessed | tf_op | source)
XLA Modules:
  0.0 84.5 jit_solution(18245545285618635416)
XLA Ops:
  0.6 82.5 %cg.1 = f32[12,1,384]{2,1,0:T(1,128)} custom-call(f32[6,1,384]{2,1,0:T(1,128)} %bitcast.9, f32[6,1,384]{2,1,0:T(1,128)} %bitcast.10, f32[1,1,192,384]{3,2,1,0:T(8,128)} %sens_hbm.1, f32[16,24,384]{2,1,0:T(8,128)} %kern_hbm.1, bf16[2,2,256,384]{3,2,1,0:T(8,128)(2,1)} %constant.4.clone.invr_hbm, bf16[2,384,384]{2,1,0:T(8,128)(2,1)} %constant.5.clone.invl_hbm, ...), custom_call_target="tpu_custom_call" | custom-call | tf_op jit(solution)/shard_map/cg/pallas_call | solution.py:676
  83.1 1.3 %slice_bitcast_fusion = (f32[1,6,384]{2,0,1:T(1,128)}, f32[1,6,384]{2,0,1:T(1,128)}) fusion(f32[12,1,384]{2,1,0:T(1,128)} %cg.1), kind=kLoop, calls=%fused_computation | loop fusion | bytes 36864 | tf_op jit(solution)/shard_map/transpose | solution.py:685
